TPU v7x, 256 devices: a whole 4x4x8 slice. The times are simulated.
256 devices in a mesh: dp: 32 (over x, z), tensor: 8 (over y, core).
Axes of the slice: x: 4, y: 4, z: 8, core: 2. Of those that a mesh axis runs over, the one named last changes fastest.
Arguments:
- activations: bfloat16 [2048, 24, 14336], P('dp', None, 'tensor'), may hold values from -6 to 6
- out_grads: bfloat16 [2048, 24, 4096], P('dp', None, 'tensor'), may hold values from -6 to 6
- proj_in: bfloat16 [14336, 64], P('tensor'), may hold values from -0.046875 to 0.046875
- proj_out: bfloat16 [4096, 64], P('tensor'), may hold values from -0.09375 to 0.09375
- queries: bfloat16 [32, 5120, 4096], P('dp', 'tensor'), may hold values from -0.09375 to 0.09375
- candidates: int32 [2048, 4], P('dp'), may hold values from 0 to 31, all different within a row; in each aligned block of 64 rows (0 to 63, 64 to 127, ...) at most 20 rows name the same one
Outputs:
- scores: float32 [2048, 4, 5120], P('dp', None, 'tensor')
Inputs may be any that keep to these rules, and one draw needn't show every extreme that they name: `candidates`: each example names 4 different groups. Among the 64 examples of one index of dp at most 20 name the same group, and in every draw some group is named by exactly 20 of them.
All inputs are finite; a program needn't handle non-finite values.
Results may differ from a plain program's by a relative error of at most 0.0029.
Values may be sent and summed in bfloat16 or wider, within the bound.
A program may use at most 64 MiB of HBM per device.

v0:
```python
import jax
import jax.numpy as jnp
from jax import lax
from jax.sharding import PartitionSpec as P

epsilon = 1e-06


def local(activations, out_grads, proj_in, proj_out, queries, candidates):
    examples_here, tokens_here, hidden_here = activations.shape
    proj_rank = proj_in.shape[1]
    per_example = candidates.shape[1]
    groups = lax.axis_size("dp")
    capacity = max(2, 5 * examples_here * per_example // (2 * groups))
    act_proj = jnp.dot(
        activations.reshape(examples_here * tokens_here, hidden_here),
        proj_in,
        preferred_element_type=jnp.float32,
    )
    grad_proj = jnp.dot(
        out_grads.reshape(examples_here * tokens_here, out_grads.shape[2]),
        proj_out,
        preferred_element_type=jnp.float32,
    )
    both_proj = jnp.concatenate([grad_proj, act_proj], axis=1).reshape(
        examples_here, tokens_here, 2 * proj_rank
    )
    summed = lax.psum(both_proj, "tensor")
    grad_side = summed[:, :, :proj_rank]
    act_side = summed[:, :, proj_rank:]
    example_grads = jnp.einsum(
        "eta,etb->eab", grad_side, act_side, precision=lax.Precision.HIGHEST
    ).reshape(examples_here, proj_rank * proj_rank)
    inv_rms = lax.rsqrt(jnp.mean(example_grads * example_grads, axis=1, keepdims=True) + epsilon)
    unit_grads = (example_grads * inv_rms).astype(jnp.bfloat16)
    flat_cands = candidates.reshape(-1)
    hit_table = (flat_cands[:, None] == jnp.arange(groups, dtype=jnp.int32)[None, :]).astype(
        jnp.int32
    )
    earlier = jnp.cumsum(hit_table, axis=0) - hit_table
    slot_index = jnp.sum(earlier * hit_table, axis=1)
    dest_index = flat_cands * capacity + slot_index
    row_copies = jnp.repeat(unit_grads, per_example, axis=0)
    grad_width = unit_grads.shape[1]
    send_buffer = (
        jnp.zeros((groups * capacity, grad_width), jnp.bfloat16).at[dest_index].set(row_copies)
    )
    send_buffer = send_buffer.reshape(groups, capacity, grad_width)
    query_block = queries[0]
    slot_scores = jnp.einsum(
        "gsk,qk->gsq",
        lax.all_to_all(send_buffer, "dp", split_axis=0, concat_axis=0, tiled=True),
        query_block,
        preferred_element_type=jnp.float32,
    )
    returned = lax.all_to_all(slot_scores, "dp", split_axis=0, concat_axis=0, tiled=True)
    picked = returned.reshape(groups * capacity, returned.shape[2])[dest_index]
    return picked.reshape(examples_here, per_example, returned.shape[2])


def solution(mesh):
    placed = (
        P("dp", None, "tensor"),
        P("dp", None, "tensor"),
        P("tensor", None),
        P("tensor", None),
        P("dp", "tensor", None),
        P("dp", None),
    )
    return jax.shard_map(
        local, mesh=mesh, in_specs=placed, out_specs=P("dp", None, "tensor"), check_vma=False
    )
```

profile of v0, /device:TPU:6, one launch (start us, length us, event | category | flops | bytes accessed | tf_op | source)
XLA Modules:
  0.0 332.7 jit_solution(5751738510498375177)
XLA Ops:
  6.5 0.0 copy-start
  6.5 0.0 all-reduce.2.cloned.1.call-start
  6.5 1.4 copy-done
  7.9 1.4 fusion.11
  9.4 0.0 copy-start.1
  9.4 4.3 %fusion.12 = f32[1536,64]{0,1:T(8,128)S(1)} fusion(bf16[1536,1792]{1,0:T(8,128)(2,1)} %bitcast.34, bf16[1792,64]{0,1:T(8,128)(2,1)} %param.8), kind=kOutput, calls=%fused_computation.26 | convolution fusion | flops 352321536 | bytes 6127616 | tf_op jit(solution)/shard_map/dot_general | solution.py:15
  13.7 0.1 pad_maximum_fusion
  13.8 1.1 copy.19
  14.9 0.0 all-reduce.2.cloned.1.call-update
  15.0 0.0 copy-done.1
  15.0 0.1 copy.16
  15.1 0.1 eq.29
  15.2 0.6 reduce-window.6
  15.8 0.2 slice_reduce_fusion
  16.0 0.1 eq.25
  16.1 0.1 copy.15
  16.2 0.1 mul.33
  16.3 0.1 fusion.9
  16.4 68.6 %all-reduce.2.cloned.1.call-done = f32[64,24,128]{2,1,0:T(8,128)} async-done(((f32[64,24,128]{2,1,0:T(8,128)}), f32[64,24,128]{2,1,0:T(8,128)}) %all-reduce.2.cloned.1.call-update) | async-done | bytes 786448 | tf_op jit(solution)/shard_map/psum | solution.py:28
  85.1 7.0 %multiply_reduce_fusion = (f32[64]{0:T(128)S(1)}, f32[64,64,64]{2,1,0:T(8,128)}) fusion(f32[64,24,128]{2,1,0:T(8,128)} %all-reduce.2.cloned.1.call-done), kind=kOutput, calls=%fused_computation.6 | convolution fusion | flops 76021696 | bytes 2621696 | tf_op jit(solution)/shard_map/eta,etb->eab/dot_general | solution.py:31
  92.0 2.1 reshape.82
  94.2 0.1 multiply_convert_fusion
  94.3 2.3 broadcast_in_dim.5
  96.6 4.0 %reshape.99 = bf16[256,4096]{1,0:T(8,128)(2,1)} reshape(bf16[64,4,4096]{2,1,0:T(4,128)(2,1)} %broadcast_in_dim.5) | data formatting | bytes 4194304 | tf_op jit(solution)/shard_map/reshape | solution.py:43
  100.6 7.7 %scatter_custom_fusion = bf16[640,4096]{1,0:T(8,128)(2,1)} fusion(s32[256]{0:T(256)S(1)} %bitcast.36, bf16[256,4096]{1,0:T(8,128)(2,1)} %reshape.99, bf16[]{:T(256)} %constant.7.clone.1), kind=kCustom, calls=%fused_computation.4 | custom fusion | bytes 5243392 | tf_op jit(solution)/shard_map/scatter | solution.py:46
  108.3 0.0 slice-start
  108.3 7.8 %reshape.84 = bf16[32,20,4096]{2,1,0:T(8,128)(2,1)} reshape(bf16[640,4096]{1,0:T(8,128)(2,1)} %scatter_custom_fusion) | data formatting | bytes 10485760 | tf_op jit(solution)/shard_map/reshape | solution.py:48
  116.1 0.0 slice-start.1
  116.1 147.1 %all_to_all.10 = bf16[32,20,4096]{2,1,0:T(8,128)(2,1)S(1)} all-to-all(bf16[32,20,4096]{2,1,0:T(8,128)(2,1)} %reshape.84), channel_id=1, replica_groups=mesh['dp'=32,'tensor'=8] {'dp'}, dimensions={0} | all-to-all | bytes 10485760 | tf_op jit(solution)/shard_map/all_to_all | solution.py:52
  263.3 0.0 slice-done
  263.3 0.0 slice-done.1
  263.3 6.5 %fusion = f32[32,20,640]{2,1,0:T(8,128)} fusion(bf16[32,20,4096]{2,1,0:T(8,128)(2,1)S(1)} %all_to_all.10, bf16[1,640,4096]{2,1,0:T(8,128)(2,1)S(1)} %bitcast.40), kind=kOutput, calls=%fused_computation.2 | convolution fusion | flops 3355443200 | bytes 12124160 | tf_op jit(solution)/shard_map/gsk,qk->gsq/dot_general | solution.py:50
  269.7 7.3 %all-to-all-start.1 = ((f32[32,20,640]{2,1,0:T(8,128)}), f32[32,20,640]{2,1,0:T(8,128)}, u32[]{:S(2)}, u32[]{:S(2)}) async-start(f32[32,20,640]{2,1,0:T(8,128)} %fusion), calls=%async_computation.1 | async-start | bytes 3932160 | tf_op jit(solution)/shard_map/all_to_all | solution.py:56
  277.1 43.1 %all-to-all-done.1 = f32[32,20,640]{2,1,0:T(8,128)} async-done(((f32[32,20,640]{2,1,0:T(8,128)}), f32[32,20,640]{2,1,0:T(8,128)}, u32[]{:S(2)}, u32[]{:S(2)}) %all-to-all-start.1) | async-done | bytes 1638432 | tf_op jit(solution)/shard_map/all_to_all | solution.py:56
  320.2 1.6 reshape.85
  321.8 1.9 gather_fusion
  323.7 2.1 reshape.86
  (8 shorter events, 0.1 us)
Async XLA Ops:
  6.5 1.4 copy-start
  6.5 78.5 %all-reduce.2.cloned.1.call-start = ((), (), s32[]{:S(2)}) async-start(), calls=%async_computation.2 | async-start | bytes 1572864 | tf_op jit(solution)/shard_map/psum | solution.py:28
  9.4 5.6 %copy-start.1 = (s32[64,4]{0,1:T(4,128)S(1)}, s32[64,4]{0,1:T(4,128)}, u32[]{:S(2)}) copy-start(s32[64,4]{0,1:T(4,128)} %param.11) | copy-start | bytes 3076
  108.3 154.9 %slice-start = ((s8[5242880]{0:T(1024)(128)(4,1)}), s8[1048576]{0:T(1024)(128)(4,1)S(1)}, s32[]{:S(2)}) async-start(s8[5242880]{0:T(1024)(128)(4,1)} %bitcast.39), calls=%async_computation.3 | async-start | bytes 2097152
  116.1 147.2 %slice-start.1 = ((s8[5242880]{0:T(1024)(128)(4,1)}), s8[4194304]{0:T(1024)(128)(4,1)S(1)}, s32[]{:S(2)}) async-start(s8[5242880]{0:T(1024)(128)(4,1)} %bitcast.39), calls=%async_computation.4 | async-start | bytes 8388608
  269.7 50.5 %all-to-all-start.1 = ((f32[32,20,640]{2,1,0:T(8,128)}), f32[32,20,640]{2,1,0:T(8,128)}, u32[]{:S(2)}, u32[]{:S(2)}) async-start(f32[32,20,640]{2,1,0:T(8,128)} %fusion), calls=%async_computation.1 | async-start | bytes 3932160 | tf_op jit(solution)/shard_map/all_to_all | solution.py:56
Sparse Core Ops, SparseCore 0:
  15.1 69.9 all-reduce.1
where the time goes:
time: 338 us; the launch traced here: 333 us
  blocking collectives  147 us (43%)
  waiting for transfers between devices  112 us (33%)
  local copies, waits for them, and re-layouts  32.8 us (10%)
  matrix products  19.2 us (6%)
  between operations  13.5 us (4%)
  starting transfers between devices  7.34 us (2%)
    all_to_all x1, blocking collectives, local(): lax.all_to_all(send_buffer, 'dp', split_axis=0, concat_axis=0, tiled=True)  147 us
    psum x1, waiting for transfers between devices, local(): summed = lax.psum(both_proj, 'tensor')  68.6 us
    all_to_all x1, waiting for transfers between devices, local(): lax.all_to_all(slot_scores, 'dp', split_axis=0, concat_axis=0, tiled=True)  43.1 us
    reshape x1, local copies, waits for them, and re-layouts, local(): send_buffer = send_buffer.reshape(groups, capacity, grad_width)  7.78 us
    scatter x1, local copies, waits for them, and re-layouts, local(): jnp.zeros((groups * capacity, grad_width), jnp.bfloat16).at[dest_index]  7.75 us
    all_to_all x1, starting transfers between devices, local(): lax.all_to_all(slot_scores, 'dp', split_axis=0, concat_axis=0, tiled=True)  7.34 us
    dot_general x1, matrix products, local(): jnp.einsum('eta,etb->eab', grad_side, act_side, precision=lax.Precision.H...  6.96 us
  transfers between devices with their start and end apart: 2, of which 2 were waited for; matrix products, arithmetic and copies ran while one was open for 0% of the time, Pallas kernels for 0%

commit v1 on v0

v1 whole, which is shorter than its diff:
```python
import jax
import jax.numpy as jnp
from jax import lax
from jax.experimental import pallas as pl
from jax.experimental.pallas import tpu as pltpu
from jax.sharding import PartitionSpec as P

EPS = 1e-06
NX, NZ, NY = 4, 8, 4
F32, BF16, I32 = jnp.float32, jnp.bfloat16, jnp.int32
NT = (((1,), (1,)), ((), ()))


def iota(shape, axis):
    return lax.broadcasted_iota(I32, shape, axis)


def main_kernel(
    act, og, pin, pout, qh, cand, ret,
    abuf, obuf, wa, wo, expand, part, rcore, csum, rrel, fin, rfin, pbuf, ubuf32, usend,
    zb, xs, r, q0, q1, rs,
    act_sem, og_sem, q_sem,
    core_s, core_r, rel_s, rel_r, fin_s, fin_r, u_s, u_r,
    z_s, z_r, x_s, x_r, y_s, y_r, c_s, c_r, b_s, b_r,
):
    dp = lax.axis_index("dp")
    t = lax.axis_index("tensor")
    x, z = dp // NZ, dp % NZ
    y, c = t // 2, t % 2

    def dev(dp_to, t_to):
        return {"dp": dp_to, "tensor": t_to}

    def rcopy(src, dst, ss, rr, to):
        return pltpu.make_async_remote_copy(
            src_ref=src, dst_ref=dst, send_sem=ss, recv_sem=rr,
            device_id=to, device_id_type=pl.DeviceIdType.MESH,
        )

    partner = dev(dp, 2 * y + (1 - c))
    yup = dev(dp, 2 * ((y + 1) % NY) + c)
    ydn = dev(dp, 2 * ((y + NY - 1) % NY) + c)
    zup = dev(x * NZ + (z + 1) % NZ, t)
    zdn = dev(x * NZ + (z + NZ - 1) % NZ, t)

    ys = [(y + 2) % NY, (y + 1) % NY, (y + 3) % NY, y]
    loads = []
    for n in range(8):
        tb = 2 * ys[n // 2] + ((1 - c) if n % 2 == 0 else c)
        rows = pl.ds(pl.multiple_of(tb * 192, 192), 192)
        a = pltpu.make_async_copy(act.at[rows, :], abuf.at[n], act_sem.at[n])
        o = pltpu.make_async_copy(og.at[rows, :], obuf.at[n], og_sem.at[n])
        a.start()
        o.start()
        loads.append((a, o))

    barrier = pltpu.get_barrier_semaphore()

    @pl.loop(1, NX * NZ)
    def _(k):
        pl.semaphore_signal(barrier, inc=1, device_id=dev((dp + k) % (NX * NZ), t),
                            device_id_type=pl.DeviceIdType.MESH)

    @pl.loop(1, 8)
    def _(k):
        pl.semaphore_signal(barrier, inc=1, device_id=dev(dp, (t + k) % 8),
                            device_id_type=pl.DeviceIdType.MESH)

    rel_y = [y, (y + 3) % NY, (y + 1) % NY, (y + 2) % NY]
    qloads = []
    for rel in range(8):
        ts = 2 * rel_y[rel // 2] + (c if rel % 2 == 0 else 1 - c)
        for h, dst in ((0, q0), (1, q1)):
            cols = pl.ds(pl.multiple_of(ts * 512 + h * 256, 256), 256)
            cp = pltpu.make_async_copy(
                qh.at[:, cols], dst.at[:, pl.ds(rel * 256, 256)], q_sem.at[2 * rel + h]
            )
            cp.start()
            qloads.append(cp)

    wa[0:64, :] = jnp.zeros((64, wa.shape[1]), BF16)
    wa[64:128, :] = pin[...]
    wo[0:64, :] = pout[...]
    wo[64:128, :] = jnp.zeros((64, wo.shape[1]), BF16)

    def project(n):
        for cp in loads[n]:
            cp.wait()
        part[n] = lax.dot_general(
            abuf[n], wa[...], NT, preferred_element_type=F32
        ) + lax.dot_general(obuf[n], wo[...], NT, preferred_element_type=F32)

    core_cp = [rcopy(part.at[2 * j], rcore.at[j], core_s.at[j], core_r.at[j], partner)
               for j in range(4)]
    rel_cp = [rcopy(csum.at[pl.ds(0, 96)], rrel.at[0], rel_s.at[0], rel_r.at[0], yup),
              rcopy(csum.at[pl.ds(96, 96)], rrel.at[1], rel_s.at[1], rel_r.at[1], ydn)]
    fin_cp = [rcopy(fin.at[0], rfin.at[0], fin_s.at[0], fin_r.at[0], yup),
              rcopy(fin.at[1], rfin.at[1], fin_s.at[1], fin_r.at[1], ydn)]

    project(0)
    pl.semaphore_wait(barrier, NX * NZ - 1 + 7)
    core_cp[0].start()
    project(1)
    project(2)
    core_cp[1].start()
    project(3)
    core_cp[0].wait_recv()
    csum[...] = part[1] + rcore[0]
    rel_cp[0].start()
    rel_cp[1].start()
    project(4)
    core_cp[2].start()
    project(5)
    project(6)
    core_cp[3].start()
    project(7)

    row = iota((256, 4096), 0)
    col = iota((256, 4096), 1)
    expand[...] = jnp.where((row % 64 == col // 64) & (row < 192), 1.0, 0.0).astype(BF16)
    e_of = iota((64, 128), 1) // 16 * 8 + iota((64, 128), 1) % 8
    dup = jnp.where(iota((64, 128), 0) == e_of, 1.0, 0.0).astype(BF16)
    c2 = jnp.dot(cand[...].astype(F32).astype(BF16), dup, preferred_element_type=F32)
    zb[0, 128:136, 0:128] = c2.astype(BF16)
    zb[0, 128:136, 128:256] = jnp.zeros((8, 128), BF16)

    core_cp[1].wait_recv()
    rel_cp[0].wait_recv()
    fin[0, 0:96] = part[3, 0:96] + rcore[1, 0:96] + rrel[0]
    fin[0, 96:192] = part[3, 96:192] + rcore[1, 96:192]
    fin_cp[0].start()
    core_cp[2].wait_recv()
    rel_cp[1].wait_recv()
    fin[1, 0:96] = part[5, 0:96] + rcore[2, 0:96]
    fin[1, 96:192] = part[5, 96:192] + rcore[2, 96:192] + rrel[1]
    fin_cp[1].start()
    core_cp[3].wait_recv()
    fin_cp[0].wait_recv()
    fin_cp[1].wait_recv()
    pbuf[...] = part[7] + rcore[3] + rfin[0] + rfin[1]

    pt = jnp.concatenate([pbuf[pl.ds(k, 8, stride=24), :] for k in range(24)], axis=0)
    lane = iota((192, 128), 1)
    low = lane < 64
    a2 = jnp.where(low, pltpu.roll(pt, 64, 1), pt)
    a4 = jnp.concatenate([a2, a2], axis=1)
    hi = pt.astype(BF16).astype(F32)
    rest = pt - hi
    mid = rest.astype(BF16).astype(F32)
    lo = rest - mid
    g3 = jnp.concatenate(
        [jnp.where(low, hi, pltpu.roll(mid, 64, 1)), jnp.where(low, lo, 0.0)], axis=1
    ).astype(BF16)
    sq = jnp.zeros((8, 256), F32)
    for m in range(16):
        gx = jnp.dot(g3, expand[:, 256 * m:256 * m + 256], preferred_element_type=F32)
        u = jnp.sum((gx * a4).reshape(24, 8, 256), axis=0)
        ubuf32[:, 256 * m:256 * m + 256] = u
        sq = sq + u * u
    inv = lax.rsqrt(jnp.sum(sq, axis=1, keepdims=True) / 4096.0 + EPS)
    for m in range(16):
        usend[m // 2, 8 * (m % 2):8 * (m % 2) + 8, :] = (
            ubuf32[:, 256 * m:256 * m + 256] * inv
        ).astype(BF16)
    my_rows = pl.ds(pl.multiple_of(t * 16, 16), 16)
    u_cp = []
    for k in range(1, 8):
        to = (t + k) % 8
        u_cp.append(rcopy(usend.at[to], zb.at[0, my_rows, :], u_s.at[k], u_r.at[k], dev(dp, to)))
        u_cp[-1].start()
    zb[0, my_rows, :] = usend[t]

    def u_in(k):
        fr = (t + 8 - k) % 8
        return rcopy(usend.at[fr], zb.at[0, pl.ds(pl.multiple_of(fr * 16, 16), 16), :],
                     u_s.at[k], u_r.at[k], dev(dp, fr))

    tri_r, tri_c = iota((128, 128), 0), iota((128, 128), 1)
    tri = jnp.where(
        ((tri_r // 8) % 2 == 0)
        & (tri_r // 16 * 8 + tri_r % 8 < tri_c // 16 * 8 + tri_c % 8), 1.0, 0.0
    ).astype(BF16)
    mr = iota((40, 128), 0)
    slot_of = jnp.where(mr < 16, mr, jnp.where(mr < 20, mr, jnp.where(mr < 24, mr - 4, mr - 24)))
    half_of = jnp.where(mr < 20, 0, 1)
    rowkey = (slot_of + 64 * half_of).astype(F32)
    half_lane = ((iota((1, 128), 1) // 8) % 2 * 64).astype(F32)

    for k in range(1, 8):
        u_in(k).wait_recv()
    for cp in qloads:
        cp.wait()

    def z_in(d):
        return rcopy(zb.at[d], zb.at[d], z_s.at[d], z_r.at[d], zup)

    z_half = [rcopy(zb.at[3, pl.ds(0, 72)], zb.at[4, pl.ds(0, 72)], z_s.at[4], z_r.at[4], zup),
              rcopy(zb.at[5, pl.ds(72, 64)], zb.at[4, pl.ds(72, 64)], z_s.at[0], z_r.at[0], zdn)]

    def z_up(d):
        return rcopy(zb.at[d], zb.at[d + 1], z_s.at[d + 1], z_r.at[d + 1], zup)

    def z_dn(d):
        n = (d + 7) % 8
        return rcopy(zb.at[d], zb.at[n], z_s.at[n], z_r.at[n], zdn)

    z_up(0).start()
    z_dn(0).start()

    def piece(i):
        half = (i + 1) // 2
        return (half * (2 * (i % 2) - 1) + 8) % 8

    def x_cp(d, k):
        return rcopy(xs.at[d, k], r.at[0, d, k], x_s.at[d, k], x_r.at[d, k],
                     dev((x + k) % NX * NZ + z, t))

    def y_cp(d, k):
        if k == 0:
            return rcopy(r.at[0, d], r.at[2, d], y_s.at[d, 0], y_r.at[d, 0], yup)
        if k == 1:
            return rcopy(r.at[0, d], r.at[4, d], y_s.at[d, 1], y_r.at[d, 1], ydn)
        if k == 2:
            return rcopy(r.at[2, d, pl.ds(0, 2)], r.at[6, d, pl.ds(0, 2)],
                         y_s.at[d, 2], y_r.at[d, 2], yup)
        return rcopy(r.at[4, d, pl.ds(2, 2)], r.at[6, d, pl.ds(2, 2)],
                     y_s.at[d, 3], y_r.at[d, 3], ydn)

    def c_cp(d, k):
        return rcopy(r.at[2 * k, d], r.at[2 * k + 1, d], c_s.at[d, k], c_r.at[d, k], partner)

    def b_cp(d, k):
        to = (x + NX - k) % NX * NZ + (z + NZ - d) % NZ
        return rcopy(rs.at[d, k], ret.at[d, k], b_s.at[d, k], b_r.at[d, k], dev(to, t))

    def own_cp():
        return pltpu.make_async_copy(rs.at[0, 0], ret.at[0, 0], b_s.at[0, 0])

    def pack(d):
        cz = zb[d, 128:136, 0:128].astype(F32)
        eqs = []
        for k in range(NX):
            g = ((x + k) % NX * NZ + z).astype(F32)
            eqs.append(jnp.where(cz == g, 1.0, 0.0))
        ranks = jnp.dot(jnp.concatenate(eqs, axis=0).astype(BF16), tri,
                        preferred_element_type=F32)
        hots = []
        for k in range(NX):
            hit = jnp.sum(eqs[k], axis=0, keepdims=True)
            rank = jnp.sum(ranks[8 * k:8 * k + 8], axis=0, keepdims=True)
            key = jnp.where(hit > 0.5, rank + half_lane, -1.0)
            hots.append(jnp.where(rowkey == key, 1.0, 0.0))
        hot = jnp.concatenate(hots, axis=0).astype(BF16)
        msg = jnp.dot(hot, zb[d, 0:128, :], preferred_element_type=F32)
        r[0, d, 0] = msg[0:40].astype(BF16)
        for k in range(1, NX):
            xs[d, k] = msg[40 * k:40 * k + 40].astype(BF16)

    row8 = iota((8, 128), 0)

    def scores(d):
        l0 = jnp.concatenate([r[k, d, :, 0:24, :].reshape(96, 256) for k in range(8)], axis=1)
        l1 = jnp.concatenate([r[k, d, :, 16:40, :].reshape(96, 256) for k in range(8)], axis=1)
        acc0 = lax.dot_general(l0, q0[...], NT, preferred_element_type=F32)
        acc1 = lax.dot_general(l1, q1[...], NT, preferred_element_type=F32)
        for k in range(NX):
            b = 24 * k
            m = acc0[b:b + 16] + acc1[b + 8:b + 24]
            ex = acc0[b + 16:b + 24] + pltpu.roll(acc1[b:b + 8], 4, 0)
            ex2 = pltpu.roll(ex, 4, 0)
            for j in range(5):
                rs[d, k, 16 * j:16 * j + 16, :] = m[:, 128 * j:128 * j + 128].astype(BF16)
            for j in range(3):
                v = ex[:, 128 * j:128 * j + 128]
                if j < 2:
                    v = jnp.where(row8 < 4, v, ex2[:, 128 * j + 384:128 * j + 512])
                rs[d, k, 80 + 8 * j:88 + 8 * j, :] = v.astype(BF16)

    @pl.loop(0, 12)
    def _(i):
        @pl.when(i < 8)
        def _():
            d = piece(i)

            @pl.when((i % 2 == 1) & (i < 7))
            def _():
                z_in(d).wait_recv()

                @pl.when(d < 3)
                def _():
                    z_up(d).start()

                @pl.when(d == 3)
                def _():
                    z_half[0].start()

            @pl.when((i % 2 == 0) & (i > 0))
            def _():
                z_in(d).wait_recv()

                @pl.when(d > 5)
                def _():
                    z_dn(d).start()

                @pl.when(d == 5)
                def _():
                    z_half[1].start()

            @pl.when(i == 7)
            def _():
                z_half[0].wait_recv()
                z_half[1].wait_recv()

            pack(d)
            for k in range(1, NX):
                x_cp(d, k).start()

        @pl.when((i >= 1) & (i < 9))
        def _():
            d = piece(i - 1)
            for k in range(1, NX):
                x_cp(d, k).wait_recv()
            y_cp(d, 0).start()
            y_cp(d, 1).start()
            c_cp(d, 0).start()

        @pl.when((i >= 2) & (i < 10))
        def _():
            d = piece(i - 2)
            y_cp(d, 0).wait_recv()
            y_cp(d, 2).start()
            y_cp(d, 1).wait_recv()
            y_cp(d, 3).start()
            c_cp(d, 1).start()
            c_cp(d, 2).start()

        @pl.when((i >= 3) & (i < 11))
        def _():
            d = piece(i - 3)
            y_cp(d, 2).wait_recv()
            y_cp(d, 3).wait_recv()
            c_cp(d, 3).start()

        @pl.when(i >= 4)
        def _():
            d = piece(i - 4)
            for k in range(4):
                c_cp(d, k).wait_recv()
            scores(d)
            for k in range(1, NX):
                b_cp(d, k).start()

            @pl.when(d > 0)
            def _():
                b_cp(d, 0).start()

            @pl.when(d == 0)
            def _():
                own_cp().start()

    for j in range(4):
        core_cp[j].wait_send()
    for j in range(2):
        rel_cp[j].wait_send()
        fin_cp[j].wait_send()
        z_half[j].wait_send()
    for cp in u_cp:
        cp.wait_send()
    for d in (1, 2, 3, 5, 6, 7):
        z_in(d).wait_send()

    @pl.loop(0, 8)
    def _(d):
        for k in range(4):
            y_cp(d, k).wait_send()
            c_cp(d, k).wait_send()
        for k in range(1, NX):
            x_cp(d, k).wait_send()
            b_cp(d, k).wait_send()
            b_cp(d, k).wait_recv()

    own_cp().wait()

    @pl.loop(1, 8)
    def _(d):
        b_cp(d, 0).wait_send()
        b_cp(d, 0).wait_recv()


def pick_kernel(rel_rows, rel_flat, ret, out):
    rel = rel_rows[...].astype(F32)
    group = iota((32, 64), 0).astype(F32)
    hit = jnp.zeros((32, 64), F32)
    for k in range(4):
        hit = hit + jnp.where(rel[k:k + 1, :] == group, 1.0, 0.0)
    tri = jnp.where(iota((64, 256), 0) < iota((64, 256), 1) % 64, 1.0, 0.0).astype(BF16)
    rank = jnp.dot(hit.astype(BF16), tri, preferred_element_type=F32)
    flat = rel_flat[...].astype(F32)
    mine = jnp.where(flat == iota((32, 256), 0).astype(F32), rank, 0.0)
    slot = jnp.sum(mine, axis=0, keepdims=True)
    key = jnp.where(slot < 15.5, flat * 16.0 + slot, -1.0)
    key0 = jnp.where(slot > 15.5, flat * 8.0 + slot - 16.0, -1.0)
    key1 = jnp.where(slot > 15.5, flat * 8.0 + slot - 12.0, -1.0)
    hot = jnp.where(iota((512, 256), 0).astype(F32) == key, 1.0, 0.0).astype(BF16)
    hot0 = jnp.where(iota((256, 256), 0).astype(F32) == key0, 1.0, 0.0).astype(BF16)
    hot1 = jnp.where(iota((256, 256), 0).astype(F32) == key1, 1.0, 0.0).astype(BF16)
    TN = (((0,), (0,)), ((), ()))
    for j in range(5):
        main = ret[:, :, 16 * j:16 * j + 16, :].reshape(512, 128)
        i = j % 3
        more = ret[:, :, 80 + 8 * i:88 + 8 * i, :].reshape(256, 128)
        res = lax.dot_general(hot, main, TN, preferred_element_type=F32) + lax.dot_general(
            hot0 if j < 3 else hot1, more, TN, preferred_element_type=F32
        )
        for k in range(4):
            out[:, k, 128 * j:128 * j + 128] = res[64 * k:64 * k + 64]


def local(activations, out_grads, proj_in, proj_out, queries, candidates):
    dp = lax.axis_index("dp")
    cand_t = jnp.pad(candidates.T, ((0, 4), (0, 0)), constant_values=-1)
    rel = (cand_t % NZ - dp % NZ + NZ) % NZ * NX + (cand_t // NZ - dp // NZ + NX) % NX
    vm = pl.BlockSpec(memory_space=pltpu.VMEM)
    hbm = pl.BlockSpec(memory_space=pl.ANY)
    dma = pltpu.SemaphoreType.DMA
    ret = pl.pallas_call(
        main_kernel,
        name="attribution",
        out_shape=jax.ShapeDtypeStruct((8, 4, 104, 128), BF16),
        in_specs=[hbm, hbm, vm, vm, hbm, vm],
        out_specs=vm,
        scratch_shapes=[
            pltpu.VMEM((8, 192, 1792), BF16),
            pltpu.VMEM((8, 192, 512), BF16),
            pltpu.VMEM((128, 1792), BF16),
            pltpu.VMEM((128, 512), BF16),
            pltpu.VMEM((256, 4096), BF16),
            pltpu.VMEM((8, 192, 128), F32),
            pltpu.VMEM((4, 192, 128), F32),
            pltpu.VMEM((192, 128), F32),
            pltpu.VMEM((2, 96, 128), F32),
            pltpu.VMEM((2, 192, 128), F32),
            pltpu.VMEM((2, 192, 128), F32),
            pltpu.VMEM((192, 128), F32),
            pltpu.VMEM((8, 4096), F32),
            pltpu.VMEM((8, 16, 256), BF16),
            pltpu.VMEM((8, 136, 256), BF16),
            pltpu.VMEM((8, 4, 40, 256), BF16),
            pltpu.VMEM((8, 8, 4, 40, 256), BF16),
            pltpu.VMEM((640, 2048), BF16),
            pltpu.VMEM((640, 2048), BF16),
            pltpu.VMEM((8, 4, 104, 128), BF16),
            dma((8,)), dma((8,)), dma((16,)),
            dma((4,)), dma((4,)), dma((2,)), dma((2,)), dma((2,)), dma((2,)), dma((8,)), dma((8,)),
            dma((8,)), dma((8,)), dma((8, 4)), dma((8, 4)), dma((8, 4)), dma((8, 4)),
            dma((8, 4)), dma((8, 4)), dma((8, 4)), dma((8, 4)),
        ],
        compiler_params=pltpu.CompilerParams(
            collective_id=0, has_side_effects=True, vmem_limit_bytes=56 * 1024 * 1024
        ),
    )(
        activations.reshape(1536, 1792), out_grads.reshape(1536, 512),
        proj_in.T, proj_out.T, queries[0], cand_t,
    )
    return pl.pallas_call(
        pick_kernel,
        name="pick",
        out_shape=jax.ShapeDtypeStruct((64, 4, 640), F32),
        in_specs=[vm, vm, vm],
        out_specs=vm,
    )(rel, rel[0:4].reshape(1, 256), ret)


def solution(mesh):
    placed = (
        P("dp", None, "tensor"),
        P("dp", None, "tensor"),
        P("tensor", None),
        P("tensor", None),
        P("dp", "tensor", None),
        P("dp", None),
    )
    return jax.shard_map(
        local, mesh=mesh, in_specs=placed, out_specs=P("dp", None, "tensor"), check_vma=False
    )
```

time: 338 us -> 88.5 us (0.26); the launches traced: 333 us -> 86.8 us
  blocking collectives: 147 us -> 0 us
  waiting for transfers between devices: 112 us -> 0 us
  Pallas kernels: 0 us -> 84.9 us
  local copies, waits for them, and re-layouts: 32.8 us -> 0.66 us
  matrix products: 19.2 us -> 0 us
  between operations: 13.5 us -> 0.02 us
  starting transfers between devices: 7.34 us -> 0 us
    all_to_all x1 -> x0, blocking collectives: 147 us -> none  [local(): lax.all_to_all(send_buffer, 'dp', split_axis=0, concat_axis=0, tiled=True)]
    pallas_call x0 -> x2, Pallas kernels: none -> 84.9 us  [the longest x1 82 us: local(): pl.pallas_call(main_kernel, name='attribution', out_shape=jax.ShapeDtypeS...]
    psum x1 -> x0, waiting for transfers between devices: 68.6 us -> none  [local(): summed = lax.psum(both_proj, 'tensor')]
    all_to_all x1 -> x0, waiting for transfers between devices: 43.1 us -> none  [local(): lax.all_to_all(slot_scores, 'dp', split_axis=0, concat_axis=0, tiled=True)]
    dot_general x4 -> x0, matrix products: 19.2 us -> none  [the longest x1 6.96 us: local(): jnp.einsum('eta,etb->eab', grad_side, act_side, precision=lax.Precision.H...]
    reshape x5 -> x1, local copies, waits for them, and re-layouts: 17.5 us -> 0.66 us  [local(): rel[0:4].reshape(1, 256)]
    scatter x1 -> x0, local copies, waits for them, and re-layouts: 7.75 us -> none  [local(): jnp.zeros((groups * capacity, grad_width), jnp.bfloat16).at[dest_index]]
    all_to_all x1 -> x0, starting transfers between devices: 7.34 us -> none  [local(): lax.all_to_all(slot_scores, 'dp', split_axis=0, concat_axis=0, tiled=True)]
  transfers between devices with their start and end apart: 2 -> 0, of which waited for: 2 -> 0; matrix products, arithmetic and copies ran while one was open for 0% -> 0% of each run, Pallas kernels for 0% -> 0%
where the time goes in v1:
time: 88.5 us; the launch traced here: 86.8 us
  Pallas kernels  84.9 us (96%)
  other arithmetic  1.28 us (1%)
    pallas_call x1, Pallas kernels, local(): pl.pallas_call(main_kernel, name='attribution', out_shape=jax.ShapeDtypeS...  82 us
    pallas_call x1, Pallas kernels, local(): pl.pallas_call(pick_kernel, name='pick', out_shape=jax.ShapeDtypeStruct((...  2.92 us

profile of v1, /device:TPU:6, one launch (start us, length us, event | category | flops | bytes accessed | tf_op | source)
XLA Modules:
  0.0 86.8 jit_solution(3402031685062478107)
XLA Ops:
  0.0 1.3 %fusion.10 = (s32[8,64]{1,0:T(8,128)}, s32[8,64]{1,0:T(8,128)S(1)}) fusion(s32[4,64]{1,0:T(4,128)} %bitcast.11, s32[]{:T(128)S(6)} %select_n.34, s32[]{:T(128)S(6)} %select_n.31), kind=kLoop, calls=%fused_computation.22 | loop fusion | flops 24064 | bytes 5128 | tf_op jit(solution)/shard_map/jit(_pad)/pad | solution.py:421
  1.3 0.0 copy-start
  1.3 0.7 reshape.9.rel_flat
  1.9 82.0 %attribution.1.ret = bf16[8,4,104,128]{3,2,1,0:T(8,128)(2,1)} custom-call(bf16[1536,1792]{1,0:T(8,128)(2,1)} %bitcast.6, bf16[1536,512]{1,0:T(8,128)(2,1)} %bitcast.8, bf16[64,1792]{1,0:T(8,128)(2,1)} %bitcast.9, bf16[64,512]{1,0:T(8,128)(2,1)} %bitcast.10, bf16[640,4096]{1,0:T(8,128)(2,1)} %bitcast.7, s32[8,64]{1,0:T(8,128)} %get-tuple-element.5.cand), custom_call_target="tpu_custom_call" | custom-call | tf_op jit(solution)/shard_map/attribution/pallas_call | solution.py:426
  83.9 0.0 copy-done
  83.9 2.9 %pick.1 = f32[64,4,640]{2,1,0:T(4,128)} custom-call(s32[8,64]{1,0:T(8,128)} %copy-done, s32[1,256]{1,0:T(1,128)} %reshape.9.rel_flat, bf16[8,4,104,128]{3,2,1,0:T(8,128)(2,1)} %attribution.1.ret), custom_call_target="tpu_custom_call" | custom-call | tf_op jit(solution)/shard_map/pick/pallas_call | solution.py:465
  (1 shorter events, 0.0 us)
Async XLA Ops:
  1.3 82.6 %copy-start = (s32[8,64]{1,0:T(8,128)}, s32[8,64]{1,0:T(8,128)S(1)}, u32[]{:S(2)}) copy-start(s32[8,64]{1,0:T(8,128)S(1)} %get-tuple-element.6.rel_rows) | copy-start | bytes 6148

commit v2 on v0

v2 whole, which is shorter than its diff:
```python
import jax
import jax.numpy as jnp
from jax import lax
from jax.experimental import pallas as pl
from jax.experimental.pallas import tpu as pltpu
from jax.sharding import PartitionSpec as P

EPS = 1e-06
NX, NZ, NY = 4, 8, 4
F32, BF16, I32 = jnp.float32, jnp.bfloat16, jnp.int32
NT = (((1,), (1,)), ((), ()))


def iota(shape, axis):
    return lax.broadcasted_iota(I32, shape, axis)


def main_kernel(
    act, og, pin, pout, qh, cand, ret,
    abuf, obuf, wa, wo, expand, part, rcore, csum, rrel, fin, rfin, pbuf, ubuf32, usend,
    zb, cb, hotb, xs, r, q0, q1, rs, tbuf,
    act_sem, og_sem, q_sem,
    cb_s, cb_r, core_s, core_r, rel_s, rel_r, fin_s, fin_r, u_s, u_r,
    z_s, z_r, x_s, x_r, y_s, y_r, c_s, c_r, b_s, b_r, t_s, t_r,
):
    dp = lax.axis_index("dp")
    t = lax.axis_index("tensor")
    x, z = dp // NZ, dp % NZ
    y, c = t // 2, t % 2

    def dev(dp_to, t_to):
        return {"dp": dp_to, "tensor": t_to}

    def rcopy(src, dst, ss, rr, to):
        return pltpu.make_async_remote_copy(
            src_ref=src, dst_ref=dst, send_sem=ss, recv_sem=rr,
            device_id=to, device_id_type=pl.DeviceIdType.MESH,
        )

    partner = dev(dp, 2 * y + (1 - c))
    yup = dev(dp, 2 * ((y + 1) % NY) + c)
    ydn = dev(dp, 2 * ((y + NY - 1) % NY) + c)
    zup = dev(x * NZ + (z + 1) % NZ, t)
    zdn = dev(x * NZ + (z + NZ - 1) % NZ, t)

    barrier = pltpu.get_barrier_semaphore()

    def greet(to):
        pl.semaphore_signal(barrier, inc=1, device_id=to, device_id_type=pl.DeviceIdType.MESH)

    for k in range(1, 8):
        greet(dev(dp, (t + k) % 8))
    for d in (1, 2, 6, 7):
        for k in range(8):
            greet(dev(x * NZ + (z + d) % NZ, (t + k) % 8))
    for d in (3, 4, 5):
        greet(dev(x * NZ + (z + d) % NZ, t))
    for k in range(1, NX):
        greet(dev((x + k) % NX * NZ + z, t))

    ys = [(y + 2) % NY, (y + 1) % NY, (y + 3) % NY, y]
    for n in range(8):
        tb = 2 * ys[n // 2] + ((1 - c) if n % 2 == 0 else c)
        rows = pl.ds(pl.multiple_of(tb * 192, 192), 192)
        a = pltpu.make_async_copy(act.at[rows, :], abuf.at[n // 2, pl.ds(n % 2 * 192, 192)], act_sem.at[n // 2])
        o = pltpu.make_async_copy(og.at[rows, :], obuf.at[n // 2, pl.ds(n % 2 * 192, 192)], og_sem.at[n // 2])
        a.start()
        o.start()

    wa[0:64, :] = jnp.zeros((64, wa.shape[1]), BF16)
    wa[64:128, :] = pin[...]
    wo[0:64, :] = pout[...]
    wo[64:128, :] = jnp.zeros((64, wo.shape[1]), BF16)

    def project(j):
        pltpu.make_async_copy(act.at[pl.ds(0, 384), :], abuf.at[j], act_sem.at[j]).wait()
        pltpu.make_async_copy(og.at[pl.ds(0, 384), :], obuf.at[j], og_sem.at[j]).wait()
        both = lax.dot_general(
            abuf[j], wa[...], NT, preferred_element_type=F32
        ) + lax.dot_general(obuf[j], wo[...], NT, preferred_element_type=F32)
        part[2 * j] = both[0:192]
        part[2 * j + 1] = both[192:384]

    core_cp = [rcopy(part.at[2 * j], rcore.at[j], core_s.at[j], core_r.at[j], partner)
               for j in range(4)]
    rel_cp = [rcopy(csum.at[pl.ds(0, 96)], rrel.at[0], rel_s.at[0], rel_r.at[0], yup),
              rcopy(csum.at[pl.ds(96, 96)], rrel.at[1], rel_s.at[1], rel_r.at[1], ydn)]
    top, low_half = pl.ds(0, 96), pl.ds(96, 96)

    def fin_copy(j, early):
        rows = (low_half if early else top) if j == 0 else (top if early else low_half)
        n = 2 * j + (0 if early else 1)
        return rcopy(fin.at[j, rows], rfin.at[j, rows], fin_s.at[n], fin_r.at[n],
                     yup if j == 0 else ydn)

    fin_cp = [fin_copy(j, early) for j in (0, 1) for early in (True, False)]

    e_of = iota((64, 128), 1) // 16 * 8 + iota((64, 128), 1) % 8
    dup = jnp.where(iota((64, 128), 0) == e_of, 1.0, 0.0).astype(BF16)
    c2 = jnp.dot(cand[...].astype(F32).astype(BF16), dup, preferred_element_type=F32)
    cb[0] = jnp.concatenate([c2, jnp.full((4, 128), -1.0, F32)], axis=0).astype(BF16)

    def cand_cp(d):
        return rcopy(cb.at[0], cb.at[d], cb_s.at[0], cb_r.at[0], dev(x * NZ + (z + d) % NZ, t))

    project(0)
    pl.semaphore_wait(barrier, 7 + 32 + 3 + NX - 1)
    core_cp[0].start()
    for d in range(1, 8):
        cand_cp(d).start()
    project(1)
    core_cp[1].start()
    core_cp[0].wait_recv()
    csum[...] = part[1] + rcore[0]
    rel_cp[0].start()
    rel_cp[1].start()
    core_cp[1].wait_recv()
    fin[0, 96:192] = part[3, 96:192] + rcore[1, 96:192]
    fin_cp[0].start()
    project(2)
    core_cp[2].start()
    project(3)
    core_cp[3].start()
    core_cp[2].wait_recv()
    fin[1, 0:96] = part[5, 0:96] + rcore[2, 0:96]
    fin_cp[2].start()

    rel_y = [y, (y + 3) % NY, (y + 1) % NY, (y + 2) % NY]
    for rel in range(8):
        ts = 2 * rel_y[rel // 2] + (c if rel % 2 == 0 else 1 - c)
        for h, dst in ((0, q0), (1, q1)):
            cols = pl.ds(pl.multiple_of(ts * 512 + h * 256, 256), 256)
            cp = pltpu.make_async_copy(
                qh.at[:, cols], dst.at[:, pl.ds(rel * 256, 256)], q_sem.at[h]
            )
            cp.start()

    row = iota((256, 4096), 0)
    col = iota((256, 4096), 1)
    expand[...] = jnp.where((row % 64 == col // 64) & (row < 192), 1.0, 0.0).astype(BF16)
    rel_cp[0].wait_recv()
    fin[0, 0:96] = part[3, 0:96] + rcore[1, 0:96] + rrel[0]
    fin_cp[1].start()
    rel_cp[1].wait_recv()
    fin[1, 96:192] = part[5, 96:192] + rcore[2, 96:192] + rrel[1]
    fin_cp[3].start()
    tri_r, tri_c = iota((128, 128), 0), iota((128, 128), 1)
    tri = jnp.where(
        ((tri_r // 8) % 2 == 0)
        & (tri_r // 16 * 8 + tri_r % 8 < tri_c // 16 * 8 + tri_c % 8), 1.0, 0.0
    ).astype(BF16)
    mr = iota((40, 128), 0)
    slot_of = jnp.where(mr < 16, mr, jnp.where(mr < 20, mr, jnp.where(mr < 24, mr - 4, mr - 24)))
    half_of = jnp.where(mr < 20, 0, 1)
    rowkey = (slot_of + 64 * half_of).astype(F32)
    half_lane = ((iota((1, 128), 1) // 8) % 2 * 64).astype(F32)

    def choose(d):
        cz = cb[d].astype(F32)
        eqs = []
        for k in range(NX):
            g = ((x + k) % NX * NZ + z).astype(F32)
            eqs.append(jnp.where(cz == g, 1.0, 0.0))
        ranks = jnp.dot(jnp.concatenate(eqs, axis=0).astype(BF16), tri,
                        preferred_element_type=F32)
        for k in range(NX):
            hit = jnp.sum(eqs[k], axis=0, keepdims=True)
            rank = jnp.sum(ranks[8 * k:8 * k + 8], axis=0, keepdims=True)
            key = jnp.where(hit > 0.5, rank + half_lane, -1.0)
            hotb[d, 40 * k:40 * k + 40, :] = jnp.where(rowkey == key, 1.0, 0.0).astype(BF16)

    cand_all = rcopy(cb.at[pl.ds(1, 7)], cb.at[pl.ds(1, 7)], cb_s.at[0], cb_r.at[0], zup)
    cand_all.wait_recv()
    for d in range(8):
        choose(d)
    core_cp[3].wait_recv()
    for cp in fin_cp:
        cp.wait_recv()
    pbuf[...] = part[7] + rcore[3] + rfin[0] + rfin[1]

    pt = jnp.concatenate([pbuf[pl.ds(k, 8, stride=24), :] for k in range(24)], axis=0)
    lane = iota((192, 128), 1)
    low = lane < 64
    a2 = jnp.where(low, pltpu.roll(pt, 64, 1), pt)
    a4 = jnp.concatenate([a2, a2], axis=1)
    hi = pt.astype(BF16).astype(F32)
    rest = pt - hi
    mid = rest.astype(BF16).astype(F32)
    lo = rest - mid
    g3 = jnp.concatenate(
        [jnp.where(low, hi, pltpu.roll(mid, 64, 1)), jnp.where(low, lo, 0.0)], axis=1
    ).astype(BF16)
    sq = jnp.zeros((8, 256), F32)
    for m in range(16):
        gx = jnp.dot(g3, expand[:, 256 * m:256 * m + 256], preferred_element_type=F32)
        u = jnp.sum((gx * a4).reshape(24, 8, 256), axis=0)
        ubuf32[:, 256 * m:256 * m + 256] = u
        sq = sq + u * u
    inv = lax.rsqrt(jnp.sum(sq, axis=1, keepdims=True) / 4096.0 + EPS)
    for m in range(16):
        usend[m // 2, 8 * (m % 2):8 * (m % 2) + 8, :] = (
            ubuf32[:, 256 * m:256 * m + 256] * inv
        ).astype(BF16)
    my_rows = pl.ds(pl.multiple_of(t * 16, 16), 16)
    zb[0, my_rows, :] = usend[t]

    def u_cp(d, k):
        to = (t + k) % 8
        return rcopy(usend.at[to], zb.at[d, my_rows, :], u_s.at[d], u_r.at[d],
                     dev(x * NZ + (z + d) % NZ, to))

    near = (0, 1, 7, 2, 6)
    for d in near:
        for k in range(8):
            if (d, k) != (0, 0):
                u_cp(d, k).start()

    def u_all(d):
        n = 7 if d == 0 else 8
        return rcopy(zb.at[d, pl.ds(0, 16 * n)], zb.at[d, pl.ds(0, 16 * n)], u_s.at[d], u_r.at[d], zup)

    def z_in(d):
        return rcopy(zb.at[d], zb.at[d], z_s.at[d], z_r.at[d], zup)

    z_half = [rcopy(zb.at[3, pl.ds(0, 64)], zb.at[4, pl.ds(0, 64)], z_s.at[4], z_r.at[4], zup),
              rcopy(zb.at[5, pl.ds(64, 64)], zb.at[4, pl.ds(64, 64)], z_s.at[0], z_r.at[0], zdn)]
    z_far = [rcopy(zb.at[2], zb.at[3], z_s.at[3], z_r.at[3], zup),
             rcopy(zb.at[6], zb.at[5], z_s.at[5], z_r.at[5], zdn)]

    def x_cp(d, k):
        return rcopy(xs.at[d, k], r.at[0, d, k], x_s.at[0], x_r.at[d],
                     dev((x + k) % NX * NZ + z, t))

    def y_cp(d, k):
        if k == 0:
            return rcopy(r.at[0, d], r.at[2, d], y_s.at[0], y_r.at[0, d], yup)
        if k == 1:
            return rcopy(r.at[0, d], r.at[4, d], y_s.at[1], y_r.at[0, d], ydn)
        if k == 2:
            return rcopy(r.at[2, d, pl.ds(0, 2)], r.at[6, d, pl.ds(0, 2)],
                         y_s.at[2], y_r.at[1, d], yup)
        return rcopy(r.at[4, d, pl.ds(2, 2)], r.at[6, d, pl.ds(2, 2)],
                     y_s.at[2], y_r.at[1, d], ydn)

    def c_cp(d, k):
        return rcopy(r.at[2 * k, d], r.at[2 * k + 1, d], c_s.at[k], c_r.at[d], partner)

    def b_cp(d, k):
        to = (x + NX - k) % NX * NZ + (z + NZ - d) % NZ
        return rcopy(rs.at[d, k], ret.at[d, k], b_s.at[1 if d == 0 else 0], b_r.at[d], dev(to, t))

    def t_cp(k):
        to = x * NZ + (z + (2 if k < 2 else NZ - 2)) % NZ
        return rcopy(rs.at[4, k], tbuf.at[k], b_s.at[0], t_r.at[k], dev(to, t))

    def t_on(k):
        to = (x + NX - k) % NX * NZ + (z + (2 if k < 2 else NZ - 2)) % NZ
        return rcopy(tbuf.at[k], ret.at[4, k], t_s.at[0], b_r.at[4], dev(to, t))

    def own_cp():
        return pltpu.make_async_copy(rs.at[0, 0], ret.at[0, 0], b_s.at[2])

    def pack(d):
        msg = jnp.dot(hotb[d], zb[d], preferred_element_type=F32)
        r[0, d, 0] = msg[0:40].astype(BF16)
        for k in range(1, NX):
            xs[d, k] = msg[40 * k:40 * k + 40].astype(BF16)

    row8 = iota((8, 128), 0)

    def scores(d):
        l0 = jnp.concatenate([r[k, d, :, 0:24, :].reshape(96, 256) for k in range(8)], axis=1)
        l1 = jnp.concatenate([r[k, d, :, 16:40, :].reshape(96, 256) for k in range(8)], axis=1)
        acc0 = lax.dot_general(l0, q0[...], NT, preferred_element_type=F32)
        acc1 = lax.dot_general(l1, q1[...], NT, preferred_element_type=F32)
        for k in range(NX):
            b = 24 * k
            m = acc0[b:b + 16] + acc1[b + 8:b + 24]
            ex = acc0[b + 16:b + 24] + pltpu.roll(acc1[b:b + 8], 4, 0)
            ex2 = pltpu.roll(ex, 4, 0)
            for j in range(5):
                rs[d, k, 16 * j:16 * j + 16, :] = m[:, 128 * j:128 * j + 128].astype(BF16)
            for j in range(3):
                v = ex[:, 128 * j:128 * j + 128]
                if j < 2:
                    v = jnp.where(row8 < 4, v, ex2[:, 128 * j + 384:128 * j + 512])
                rs[d, k, 80 + 8 * j:88 + 8 * j, :] = v.astype(BF16)

    def s1(d):
        pack(d)
        for k in range(1, NX):
            x_cp(d, k).start()

    def s2(d):
        rcopy(r.at[0, d, pl.ds(1, 3)], r.at[0, d, pl.ds(1, 3)], x_s.at[0], x_r.at[d], zup).wait_recv()
        y_cp(d, 0).start()
        y_cp(d, 1).start()
        c_cp(d, 0).start()

    def s3(d):
        rcopy(r.at[pl.ds(0, 2), d], r.at[pl.ds(0, 2), d], y_s.at[0], y_r.at[0, d], zup).wait_recv()
        y_cp(d, 2).start()
        y_cp(d, 3).start()
        c_cp(d, 1).start()
        c_cp(d, 2).start()

    def s4(d):
        rcopy(r.at[6, d], r.at[6, d], y_s.at[2], y_r.at[1, d], zup).wait_recv()
        c_cp(d, 3).start()

    def s5(d):
        rcopy(r.at[pl.ds(0, 4), d], r.at[pl.ds(0, 4), d], c_s.at[0], c_r.at[d], zup).wait_recv()
        scores(d)
        for k in range(NX):
            if d == 4:
                t_cp(k).start()
            elif (d, k) == (0, 0):
                own_cp().start()
            else:
                b_cp(d, k).start()

    def u_wait(d):
        u_all(d).wait_recv()

    for d in near:
        u_wait(d)
        if d == 2:
            z_far[0].start()
        if d == 6:
            z_far[1].start()
        s1(d)
    for h, dst in ((0, q0), (1, q1)):
        pltpu.make_async_copy(qh.at[:, pl.ds(0, 2048)], dst, q_sem.at[h]).wait()
    s2(1)
    z_far[0].wait_recv()
    z_half[0].start()
    s1(3)
    z_far[1].wait_recv()
    z_half[1].start()
    s1(5)
    s2(6), s3(1), s2(3)
    z_half[0].wait_recv()
    z_half[1].wait_recv()
    s1(4)
    s3(6), s2(5)
    s4(1), s3(3), s5(1), s2(4)
    s4(6), s3(5), s2(2), s5(6)
    s4(3), s3(4), s2(7), s5(3)
    s4(5), s3(2), s2(0), s4(4), s5(5)
    s3(7), s4(2), s5(4)
    s3(0), s4(7), s5(2)
    s4(0), s5(7)

    def relay(ks):
        for k in ks:
            t_cp(k).wait_recv()
            t_on(k).start()

    relay((2, 3))
    s5(0)
    relay((0, 1))

    def sent():
        for j in range(4):
            core_cp[j].wait_send()
            fin_cp[j].wait_send()
        for j in range(2):
            rel_cp[j].wait_send()
            z_half[j].wait_send()
        for d in near:
            u_all(d).wait_send()
        cand_all.wait_send()
        for cp in z_far:
            cp.wait_send()

        rcopy(xs.at[:, pl.ds(1, 3)], xs.at[:, pl.ds(1, 3)], x_s.at[0], x_r.at[0], zup).wait_send()
        for k in range(3):
            rcopy(r.at[k], r.at[k], y_s.at[k], y_r.at[0, 0], zup).wait_send()
        for k in range(4):
            rcopy(r.at[k], r.at[k], c_s.at[k], c_r.at[0], zup).wait_send()

    sent()

    def got(d):
        if d == 0:
            own_cp().wait()
            some = ret.at[0, pl.ds(1, 3)]
        else:
            some = ret.at[d]
        rcopy(some, some, b_s.at[0], b_r.at[d], zup).wait_recv()

    for d in (1, 6, 3, 5, 2, 7, 0, 4):
        got(d)

    def returned():
        some = rs.at[pl.ds(1, 7)]
        rcopy(some, some, b_s.at[0], b_r.at[1], zup).wait_send()
        some = rs.at[0, pl.ds(1, 3)]
        rcopy(some, some, b_s.at[1], b_r.at[0], zup).wait_send()
        rcopy(tbuf, tbuf, t_s.at[0], t_r.at[0], zup).wait_send()

    returned()


def pick_kernel(cand, ret, out):
    dp = lax.axis_index("dp")
    cd = cand[...]
    rel = ((cd % NZ - dp % NZ + NZ) % NZ * NX + (cd // NZ - dp // NZ + NX) % NX).astype(F32)
    group = iota((32, 64), 0).astype(F32)
    hit = jnp.zeros((32, 64), F32)
    for k in range(4):
        hit = hit + jnp.where(rel[k:k + 1, :] == group, 1.0, 0.0)
    tri = jnp.where(iota((64, 256), 0) < iota((64, 256), 1) % 64, 1.0, 0.0).astype(BF16)
    rank = jnp.dot(hit.astype(BF16), tri, preferred_element_type=F32)
    lane = iota((64, 256), 1)
    dup = jnp.where(iota((64, 256), 0) == lane % 64, 1.0, 0.0).astype(BF16)
    wide = jnp.dot(rel.astype(BF16), dup, preferred_element_type=F32)
    flat = jnp.sum(jnp.where(iota((4, 256), 0) == iota((4, 256), 1) // 64, wide, 0.0),
                   axis=0, keepdims=True)
    mine = jnp.where(flat == iota((32, 256), 0).astype(F32), rank, 0.0)
    slot = jnp.sum(mine, axis=0, keepdims=True)
    rows = jnp.concatenate([flat, slot, jnp.zeros((6, 256), F32)], axis=0).astype(BF16)
    eye = jnp.where(iota((8, 128), 0) == iota((8, 128), 1), 1.0, 0.0).astype(BF16)
    cols = lax.dot_general(rows, eye, (((0,), (0,)), ((), ())), preferred_element_type=F32)
    relc, slotc = cols[:, 0:1], cols[:, 1:2]
    key = jnp.where(slotc < 15.5, relc * 16.0 + slotc, -1.0)
    key0 = jnp.where(slotc > 15.5, relc * 8.0 + slotc - 16.0, -1.0)
    key1 = jnp.where(slotc > 15.5, relc * 8.0 + slotc - 12.0, -1.0)
    at512 = iota((256, 512), 1).astype(F32)
    at256 = iota((256, 256), 1).astype(F32)
    hot = jnp.where(at512 == key, 1.0, 0.0).astype(BF16)
    hot0 = jnp.where(at256 == key0, 1.0, 0.0).astype(BF16)
    hot1 = jnp.where(at256 == key1, 1.0, 0.0).astype(BF16)
    for js, more in (((0, 1, 2), hot0), ((3, 4), hot1)):
        pick = jnp.concatenate([hot, more], axis=1)
        vals = jnp.concatenate(
            [jnp.concatenate([
                ret[:, :, 16 * j:16 * j + 16, :].reshape(512, 128),
                ret[:, :, 80 + 8 * (j % 3):88 + 8 * (j % 3), :].reshape(256, 128),
            ], axis=0) for j in js], axis=1)
        res = jnp.dot(pick, vals, preferred_element_type=F32)
        for k in range(4):
            out[:, k, 128 * js[0]:128 * js[-1] + 128] = res[64 * k:64 * k + 64]


def local(activations, out_grads, proj_in, proj_out, queries, candidates):
    cand_t = candidates.T
    vm = pl.BlockSpec(memory_space=pltpu.VMEM)
    hbm = pl.BlockSpec(memory_space=pl.ANY)
    dma = pltpu.SemaphoreType.DMA
    ret = pl.pallas_call(
        main_kernel,
        name="attribution",
        out_shape=jax.ShapeDtypeStruct((8, 4, 104, 128), BF16),
        in_specs=[hbm, hbm, vm, vm, hbm, vm],
        out_specs=hbm,
        scratch_shapes=[
            pltpu.VMEM((4, 384, 1792), BF16),
            pltpu.VMEM((4, 384, 512), BF16),
            pltpu.VMEM((128, 1792), BF16),
            pltpu.VMEM((128, 512), BF16),
            pltpu.VMEM((256, 4096), BF16),
            pltpu.VMEM((8, 192, 128), F32),
            pltpu.VMEM((4, 192, 128), F32),
            pltpu.VMEM((192, 128), F32),
            pltpu.VMEM((2, 96, 128), F32),
            pltpu.VMEM((2, 192, 128), F32),
            pltpu.VMEM((2, 192, 128), F32),
            pltpu.VMEM((192, 128), F32),
            pltpu.VMEM((8, 4096), F32),
            pltpu.VMEM((8, 16, 256), BF16),
            pltpu.VMEM((8, 128, 256), BF16),
            pltpu.VMEM((8, 8, 128), BF16),
            pltpu.VMEM((8, 160, 128), BF16),
            pltpu.VMEM((8, 4, 40, 256), BF16),
            pltpu.VMEM((8, 8, 4, 40, 256), BF16),
            pltpu.VMEM((640, 2048), BF16),
            pltpu.VMEM((640, 2048), BF16),
            pltpu.VMEM((8, 4, 104, 128), BF16),
            pltpu.VMEM((4, 104, 128), BF16),
            dma((4,)), dma((4,)), dma((2,)),
            dma((1,)), dma((1,)), dma((4,)), dma((4,)), dma((2,)), dma((2,)), dma((4,)), dma((4,)),
            dma((8,)), dma((8,)), dma((8,)), dma((8,)), dma((1,)), dma((8,)), dma((3,)), dma((2, 8)),
            dma((4,)), dma((8,)), dma((3,)), dma((8,)), dma((1,)), dma((4,)),
        ],
        compiler_params=pltpu.CompilerParams(
            collective_id=0, has_side_effects=True, vmem_limit_bytes=56 * 1024 * 1024
        ),
    )(
        activations.reshape(1536, 1792), out_grads.reshape(1536, 512),
        proj_in.T, proj_out.T, queries[0], cand_t,
    )
    return pl.pallas_call(
        pick_kernel,
        name="pick",
        out_shape=jax.ShapeDtypeStruct((64, 4, 640), F32),
        in_specs=[vm, vm],
        out_specs=vm,
    )(cand_t, ret)


def solution(mesh):
    placed = (
        P("dp", None, "tensor"),
        P("dp", None, "tensor"),
        P("tensor", None),
        P("tensor", None),
        P("dp", "tensor", None),
        P("dp", None),
    )
    return jax.shard_map(
        local, mesh=mesh, in_specs=placed, out_specs=P("dp", None, "tensor"), check_vma=False
    )
```

time: 338 us -> 72.2 us (0.21); the launches traced: 333 us -> 72.1 us
  blocking collectives: 147 us -> 0 us
  waiting for transfers between devices: 112 us -> 0 us
  Pallas kernels: 0 us -> 72.1 us
  local copies, waits for them, and re-layouts: 32.8 us -> 0 us
  matrix products: 19.2 us -> 0 us
  between operations: 13.5 us -> 0.01 us
  starting transfers between devices: 7.34 us -> 0 us
    all_to_all x1 -> x0, blocking collectives: 147 us -> none  [local(): lax.all_to_all(send_buffer, 'dp', split_axis=0, concat_axis=0, tiled=True)]
    pallas_call x0 -> x2, Pallas kernels: none -> 72.1 us  [the longest x1 69 us: local(): pl.pallas_call(main_kernel, name='attribution', out_shape=jax.ShapeDtypeS...]
    psum x1 -> x0, waiting for transfers between devices: 68.6 us -> none  [local(): summed = lax.psum(both_proj, 'tensor')]
    all_to_all x1 -> x0, waiting for transfers between devices: 43.1 us -> none  [local(): lax.all_to_all(slot_scores, 'dp', split_axis=0, concat_axis=0, tiled=True)]
    dot_general x4 -> x0, matrix products: 19.2 us -> none  [the longest x1 6.96 us: local(): jnp.einsum('eta,etb->eab', grad_side, act_side, precision=lax.Precision.H...]
    reshape x5 -> x0, local copies, waits for them, and re-layouts: 17.5 us -> none  [the longest x1 7.78 us: local(): send_buffer = send_buffer.reshape(groups, capacity, grad_width)]
    scatter x1 -> x0, local copies, waits for them, and re-layouts: 7.75 us -> none  [local(): jnp.zeros((groups * capacity, grad_width), jnp.bfloat16).at[dest_index]]
    all_to_all x1 -> x0, starting transfers between devices: 7.34 us -> none  [local(): lax.all_to_all(slot_scores, 'dp', split_axis=0, concat_axis=0, tiled=True)]
  transfers between devices with their start and end apart: 2 -> 0, of which waited for: 2 -> 0; matrix products, arithmetic and copies ran while one was open for 0% -> 0% of each run, Pallas kernels for 0% -> 0%
where the time goes in v2:
time: 72.2 us; the launch traced here: 72.1 us
  Pallas kernels  72.1 us (100%)
    pallas_call x1, Pallas kernels, local(): pl.pallas_call(main_kernel, name='attribution', out_shape=jax.ShapeDtypeS...  69 us
    pallas_call x1, Pallas kernels, local(): pl.pallas_call(pick_kernel, name='pick', out_shape=jax.ShapeDtypeStruct((...  3.12 us

profile of v2, /device:TPU:6, one launch (start us, length us, event | category | flops | bytes accessed | tf_op | source)
XLA Modules:
  0.0 72.1 jit_solution(13418134593472580421)
XLA Ops:
  0.0 69.0 %attribution.1.ret = bf16[8,4,104,128]{3,2,1,0:T(8,128)(2,1)} custom-call(bf16[1536,1792]{1,0:T(8,128)(2,1)} %bitcast.6, bf16[1536,512]{1,0:T(8,128)(2,1)} %bitcast.8, bf16[64,1792]{1,0:T(8,128)(2,1)} %bitcast.9, bf16[64,512]{1,0:T(8,128)(2,1)} %bitcast.10, bf16[640,4096]{1,0:T(8,128)(2,1)} %bitcast.7, s32[4,64]{1,0:T(4,128)} %bitcast.11), custom_call_target="tpu_custom_call" | custom-call | tf_op jit(solution)/shard_map/attribution/pallas_call | solution.py:451
  69.0 3.1 %pick.1 = f32[64,4,640]{2,1,0:T(4,128)} custom-call(s32[4,64]{1,0:T(4,128)} %bitcast.12, bf16[8,4,104,128]{3,2,1,0:T(8,128)(2,1)} %attribution.1.ret), custom_call_target="tpu_custom_call" | custom-call | tf_op jit(solution)/shard_map/pick/pallas_call | solution.py:493

commit v3 on v2

--- a/solution.py
+++ b/solution.py
@@ -19,7 +19,7 @@
     act, og, pin, pout, qh, cand, ret,
     abuf, obuf, wa, wo, expand, part, rcore, csum, rrel, fin, rfin, pbuf, ubuf32, usend,
     zb, cb, hotb, xs, r, q0, q1, rs, tbuf,
-    act_sem, og_sem, q_sem,
+    cbuf, act_sem, og_sem, q_sem, w_sem,
     cb_s, cb_r, core_s, core_r, rel_s, rel_r, fin_s, fin_r, u_s, u_r,
     z_s, z_r, x_s, x_r, y_s, y_r, c_s, c_r, b_s, b_r, t_s, t_r,
 ):
@@ -59,22 +59,35 @@
         greet(dev((x + k) % NX * NZ + z, t))
 
     ys = [(y + 2) % NY, (y + 1) % NY, (y + 3) % NY, y]
-    for n in range(8):
-        tb = 2 * ys[n // 2] + ((1 - c) if n % 2 == 0 else c)
-        rows = pl.ds(pl.multiple_of(tb * 192, 192), 192)
-        a = pltpu.make_async_copy(act.at[rows, :], abuf.at[n // 2, pl.ds(n % 2 * 192, 192)], act_sem.at[n // 2])
-        o = pltpu.make_async_copy(og.at[rows, :], obuf.at[n // 2, pl.ds(n % 2 * 192, 192)], og_sem.at[n // 2])
-        a.start()
-        o.start()
+
+    def load(j):
+        for n in (2 * j, 2 * j + 1):
+            tb = 2 * ys[j] + ((1 - c) if n % 2 == 0 else c)
+            rows = pl.ds(pl.multiple_of(tb * 192, 192), 192)
+            part_rows = pl.ds(n % 2 * 192, 192)
+            pltpu.make_async_copy(act.at[rows, :], abuf.at[j, part_rows], act_sem.at[j]).start()
+            pltpu.make_async_copy(og.at[rows, :], obuf.at[j, part_rows], og_sem.at[j]).start()
+
+    small = [
+        pltpu.make_async_copy(pin, wa.at[pl.ds(64, 64)], w_sem.at[0]),
+        pltpu.make_async_copy(pout, wo.at[pl.ds(0, 64)], w_sem.at[1]),
+        pltpu.make_async_copy(cand, cbuf, w_sem.at[2]),
+    ]
+    for cp in small:
+        cp.start()
+    load(0)
+    load(1)
 
     wa[0:64, :] = jnp.zeros((64, wa.shape[1]), BF16)
-    wa[64:128, :] = pin[...]
-    wo[0:64, :] = pout[...]
     wo[64:128, :] = jnp.zeros((64, wo.shape[1]), BF16)
+    small[0].wait()
+    small[1].wait()
 
     def project(j):
         pltpu.make_async_copy(act.at[pl.ds(0, 384), :], abuf.at[j], act_sem.at[j]).wait()
         pltpu.make_async_copy(og.at[pl.ds(0, 384), :], obuf.at[j], og_sem.at[j]).wait()
+        if j < 2:
+            load(j + 2)
         both = lax.dot_general(
             abuf[j], wa[...], NT, preferred_element_type=F32
         ) + lax.dot_general(obuf[j], wo[...], NT, preferred_element_type=F32)
@@ -95,30 +108,31 @@
 
     fin_cp = [fin_copy(j, early) for j in (0, 1) for early in (True, False)]
 
-    e_of = iota((64, 128), 1) // 16 * 8 + iota((64, 128), 1) % 8
-    dup = jnp.where(iota((64, 128), 0) == e_of, 1.0, 0.0).astype(BF16)
-    c2 = jnp.dot(cand[...].astype(F32).astype(BF16), dup, preferred_element_type=F32)
-    cb[0] = jnp.concatenate([c2, jnp.full((4, 128), -1.0, F32)], axis=0).astype(BF16)
-
     def cand_cp(d):
         return rcopy(cb.at[0], cb.at[d], cb_s.at[0], cb_r.at[0], dev(x * NZ + (z + d) % NZ, t))
 
     project(0)
     pl.semaphore_wait(barrier, 7 + 32 + 3 + NX - 1)
     core_cp[0].start()
-    for d in range(1, 8):
-        cand_cp(d).start()
     project(1)
     core_cp[1].start()
     core_cp[0].wait_recv()
     csum[...] = part[1] + rcore[0]
     rel_cp[0].start()
     rel_cp[1].start()
+    small[2].wait()
+    e_of = iota((64, 128), 1) // 16 * 8 + iota((64, 128), 1) % 8
+    dup = jnp.where(iota((64, 128), 0) == e_of, 1.0, 0.0).astype(BF16)
+    c2 = jnp.dot(cbuf[...].astype(F32).astype(BF16), dup, preferred_element_type=F32)
+    cb[0] = jnp.concatenate([c2, jnp.full((4, 128), -1.0, F32)], axis=0).astype(BF16)
+
+    for d in range(1, 8):
+        cand_cp(d).start()
+    project(2)
+    core_cp[2].start()
     core_cp[1].wait_recv()
     fin[0, 96:192] = part[3, 96:192] + rcore[1, 96:192]
     fin_cp[0].start()
-    project(2)
-    core_cp[2].start()
     project(3)
     core_cp[3].start()
     core_cp[2].wait_recv()
@@ -288,7 +302,7 @@
 
     def s1(d):
         pack(d)
-        for k in range(1, NX):
+        for k in (2, 1, 3):
             x_cp(d, k).start()
 
     def s2(d):
@@ -452,7 +466,7 @@
         main_kernel,
         name="attribution",
         out_shape=jax.ShapeDtypeStruct((8, 4, 104, 128), BF16),
-        in_specs=[hbm, hbm, vm, vm, hbm, vm],
+        in_specs=[hbm] * 6,
         out_specs=hbm,
         scratch_shapes=[
             pltpu.VMEM((4, 384, 1792), BF16),
@@ -478,7 +492,8 @@
             pltpu.VMEM((640, 2048), BF16),
             pltpu.VMEM((8, 4, 104, 128), BF16),
             pltpu.VMEM((4, 104, 128), BF16),
-            dma((4,)), dma((4,)), dma((2,)),
+            pltpu.VMEM((4, 64), I32),
+            dma((4,)), dma((4,)), dma((2,)), dma((3,)),
             dma((1,)), dma((1,)), dma((4,)), dma((4,)), dma((2,)), dma((2,)), dma((4,)), dma((4,)),
             dma((8,)), dma((8,)), dma((8,)), dma((8,)), dma((1,)), dma((8,)), dma((3,)), dma((2, 8)),
             dma((4,)), dma((8,)), dma((3,)), dma((8,)), dma((1,)), dma((4,)),

time: 72.2 us -> 70 us (0.970)
  Pallas kernels: 72.1 us -> 69.3 us
    pallas_call x1, Pallas kernels: 69 us -> 66.2 us  [local(): pl.pallas_call(main_kernel, name='attribution', out_shape=jax.ShapeDtypeS...]
where the time goes in v3:
time: 70 us; the launch traced here: 69.3 us
  Pallas kernels  69.3 us (99%)
    pallas_call x1, Pallas kernels, local(): pl.pallas_call(main_kernel, name='attribution', out_shape=jax.ShapeDtypeS...  66.2 us
    pallas_call x1, Pallas kernels, local(): pl.pallas_call(pick_kernel, name='pick', out_shape=jax.ShapeDtypeStruct((...  3.12 us

profile of v3, /device:TPU:6, one launch (start us, length us, event | category | flops | bytes accessed | tf_op | source)
XLA Modules:
  0.0 69.3 jit_solution(14792851188213813759)
XLA Ops:
  0.0 66.2 %attribution.1.ret = bf16[8,4,104,128]{3,2,1,0:T(8,128)(2,1)} custom-call(bf16[1536,1792]{1,0:T(8,128)(2,1)} %bitcast.6, bf16[1536,512]{1,0:T(8,128)(2,1)} %bitcast.8, bf16[64,1792]{1,0:T(8,128)(2,1)} %bitcast.9, bf16[64,512]{1,0:T(8,128)(2,1)} %bitcast.10, bf16[640,4096]{1,0:T(8,128)(2,1)} %bitcast.7, s32[4,64]{1,0:T(4,128)} %bitcast.11), custom_call_target="tpu_custom_call" | custom-call | tf_op jit(solution)/shard_map/attribution/pallas_call | solution.py:465
  66.2 3.1 %pick.1 = f32[64,4,640]{2,1,0:T(4,128)} custom-call(s32[4,64]{1,0:T(4,128)} %bitcast.12, bf16[8,4,104,128]{3,2,1,0:T(8,128)(2,1)} %attribution.1.ret), custom_call_target="tpu_custom_call" | custom-call | tf_op jit(solution)/shard_map/pick/pallas_call | solution.py:508

commit v4 on v3

--- a/solution.py
+++ b/solution.py
@@ -94,16 +94,16 @@
         part[2 * j] = both[0:192]
         part[2 * j + 1] = both[192:384]
 
-    core_cp = [rcopy(part.at[2 * j], rcore.at[j], core_s.at[j], core_r.at[j], partner)
+    core_cp = [rcopy(part.at[2 * j], rcore.at[j], core_s.at[0], core_r.at[j], partner)
                for j in range(4)]
     rel_cp = [rcopy(csum.at[pl.ds(0, 96)], rrel.at[0], rel_s.at[0], rel_r.at[0], yup),
-              rcopy(csum.at[pl.ds(96, 96)], rrel.at[1], rel_s.at[1], rel_r.at[1], ydn)]
+              rcopy(csum.at[pl.ds(96, 96)], rrel.at[1], rel_s.at[0], rel_r.at[1], ydn)]
     top, low_half = pl.ds(0, 96), pl.ds(96, 96)
 
     def fin_copy(j, early):
         rows = (low_half if early else top) if j == 0 else (top if early else low_half)
         n = 2 * j + (0 if early else 1)
-        return rcopy(fin.at[j, rows], rfin.at[j, rows], fin_s.at[n], fin_r.at[n],
+        return rcopy(fin.at[j, rows], rfin.at[j, rows], fin_s.at[0], fin_r.at[n],
                      yup if j == 0 else ydn)
 
     fin_cp = [fin_copy(j, early) for j in (0, 1) for early in (True, False)]
@@ -218,12 +218,13 @@
     my_rows = pl.ds(pl.multiple_of(t * 16, 16), 16)
     zb[0, my_rows, :] = usend[t]
 
+    near = (0, 1, 7, 2, 6)
+
     def u_cp(d, k):
         to = (t + k) % 8
-        return rcopy(usend.at[to], zb.at[d, my_rows, :], u_s.at[d], u_r.at[d],
+        return rcopy(usend.at[to], zb.at[d, my_rows, :], u_s.at[min(d, 1)], u_r.at[near.index(d)],
                      dev(x * NZ + (z + d) % NZ, to))
 
-    near = (0, 1, 7, 2, 6)
     for d in near:
         for k in range(8):
             if (d, k) != (0, 0):
@@ -231,15 +232,13 @@
 
     def u_all(d):
         n = 7 if d == 0 else 8
-        return rcopy(zb.at[d, pl.ds(0, 16 * n)], zb.at[d, pl.ds(0, 16 * n)], u_s.at[d], u_r.at[d], zup)
-
-    def z_in(d):
-        return rcopy(zb.at[d], zb.at[d], z_s.at[d], z_r.at[d], zup)
-
-    z_half = [rcopy(zb.at[3, pl.ds(0, 64)], zb.at[4, pl.ds(0, 64)], z_s.at[4], z_r.at[4], zup),
-              rcopy(zb.at[5, pl.ds(64, 64)], zb.at[4, pl.ds(64, 64)], z_s.at[0], z_r.at[0], zdn)]
-    z_far = [rcopy(zb.at[2], zb.at[3], z_s.at[3], z_r.at[3], zup),
-             rcopy(zb.at[6], zb.at[5], z_s.at[5], z_r.at[5], zdn)]
+        return rcopy(zb.at[d, pl.ds(0, 16 * n)], zb.at[d, pl.ds(0, 16 * n)],
+                     u_s.at[min(d, 1)], u_r.at[near.index(d)], zup)
+
+    z_half = [rcopy(zb.at[3, pl.ds(0, 64)], zb.at[4, pl.ds(0, 64)], z_s.at[0], z_r.at[0], zup),
+              rcopy(zb.at[5, pl.ds(64, 64)], zb.at[4, pl.ds(64, 64)], z_s.at[1], z_r.at[1], zdn)]
+    z_far = [rcopy(zb.at[2], zb.at[3], z_s.at[2], z_r.at[2], zup),
+             rcopy(zb.at[6], zb.at[5], z_s.at[3], z_r.at[3], zdn)]
 
     def x_cp(d, k):
         return rcopy(xs.at[d, k], r.at[0, d, k], x_s.at[0], x_r.at[d],
@@ -375,14 +374,13 @@
     relay((0, 1))
 
     def sent():
-        for j in range(4):
-            core_cp[j].wait_send()
-            fin_cp[j].wait_send()
+        rcopy(rcore, rcore, core_s.at[0], core_r.at[0], zup).wait_send()
+        rcopy(fin, fin, fin_s.at[0], fin_r.at[0], zup).wait_send()
+        rcopy(csum, csum, rel_s.at[0], rel_r.at[0], zup).wait_send()
         for j in range(2):
-            rel_cp[j].wait_send()
             z_half[j].wait_send()
-        for d in near:
-            u_all(d).wait_send()
+        u_all(0).wait_send()
+        rcopy(zb.at[pl.ds(0, 4)], zb.at[pl.ds(0, 4)], u_s.at[1], u_r.at[0], zup).wait_send()
         cand_all.wait_send()
         for cp in z_far:
             cp.wait_send()
@@ -494,8 +492,8 @@
             pltpu.VMEM((4, 104, 128), BF16),
             pltpu.VMEM((4, 64), I32),
             dma((4,)), dma((4,)), dma((2,)), dma((3,)),
-            dma((1,)), dma((1,)), dma((4,)), dma((4,)), dma((2,)), dma((2,)), dma((4,)), dma((4,)),
-            dma((8,)), dma((8,)), dma((8,)), dma((8,)), dma((1,)), dma((8,)), dma((3,)), dma((2, 8)),
+            dma((1,)), dma((1,)), dma((1,)), dma((4,)), dma((1,)), dma((2,)), dma((1,)), dma((4,)),
+            dma((2,)), dma((5,)), dma((4,)), dma((4,)), dma((1,)), dma((8,)), dma((3,)), dma((2, 8)),
             dma((4,)), dma((8,)), dma((3,)), dma((8,)), dma((1,)), dma((4,)),
         ],
         compiler_params=pltpu.CompilerParams(

time: 70 us -> 70.2 us (level)
  no operation moved by 1% of the time
where the time goes in v4:
time: 70.2 us; the launch traced here: 69.7 us
  Pallas kernels  69.7 us (99%)
    pallas_call x1, Pallas kernels, local(): pl.pallas_call(main_kernel, name='attribution', out_shape=jax.ShapeDtypeS...  66.6 us
    pallas_call x1, Pallas kernels, local(): pl.pallas_call(pick_kernel, name='pick', out_shape=jax.ShapeDtypeStruct((...  3.12 us

profile of v4, /device:TPU:6, one launch (start us, length us, event | category | flops | bytes accessed | tf_op | source)
XLA Modules:
  0.0 69.7 jit_solution(13670216173291211935)
XLA Ops:
  0.0 66.6 %attribution.1.ret = bf16[8,4,104,128]{3,2,1,0:T(8,128)(2,1)} custom-call(bf16[1536,1792]{1,0:T(8,128)(2,1)} %bitcast.6, bf16[1536,512]{1,0:T(8,128)(2,1)} %bitcast.8, bf16[64,1792]{1,0:T(8,128)(2,1)} %bitcast.9, bf16[64,512]{1,0:T(8,128)(2,1)} %bitcast.10, bf16[640,4096]{1,0:T(8,128)(2,1)} %bitcast.7, s32[4,64]{1,0:T(4,128)} %bitcast.11), custom_call_target="tpu_custom_call" | custom-call | tf_op jit(solution)/shard_map/attribution/pallas_call | solution.py:463
  66.6 3.1 %pick.1 = f32[64,4,640]{2,1,0:T(4,128)} custom-call(s32[4,64]{1,0:T(4,128)} %bitcast.12, bf16[8,4,104,128]{3,2,1,0:T(8,128)(2,1)} %attribution.1.ret), custom_call_target="tpu_custom_call" | custom-call | tf_op jit(solution)/shard_map/pick/pallas_call | solution.py:506

commit v5 on v4

--- a/solution.py
+++ b/solution.py
@@ -362,16 +362,14 @@
     s4(5), s3(2), s2(0), s4(4), s5(5)
     s3(7), s4(2), s5(4)
     s3(0), s4(7), s5(2)
-    s4(0), s5(7)
+    s4(0), s5(7), s5(0)
 
     def relay(ks):
         for k in ks:
             t_cp(k).wait_recv()
             t_on(k).start()
 
-    relay((2, 3))
-    s5(0)
-    relay((0, 1))
+    relay((2, 3, 0, 1))
 
     def sent():
         rcopy(rcore, rcore, core_s.at[0], core_r.at[0], zup).wait_send()

time: 70.2 us -> 70.2 us (level)
  no operation moved by 1% of the time
where the time goes in v5:
time: 70.2 us; the launch traced here: 69.7 us
  Pallas kernels  69.7 us (99%)
    pallas_call x1, Pallas kernels, local(): pl.pallas_call(main_kernel, name='attribution', out_shape=jax.ShapeDtypeS...  66.6 us
    pallas_call x1, Pallas kernels, local(): pl.pallas_call(pick_kernel, name='pick', out_shape=jax.ShapeDtypeStruct((...  3.12 us

profile of v5, /device:TPU:6, one launch (start us, length us, event | category | flops | bytes accessed | tf_op | source)
XLA Modules:
  0.0 69.7 jit_solution(2500411137099350271)
XLA Ops:
  0.0 66.6 %attribution.1.ret = bf16[8,4,104,128]{3,2,1,0:T(8,128)(2,1)} custom-call(bf16[1536,1792]{1,0:T(8,128)(2,1)} %bitcast.6, bf16[1536,512]{1,0:T(8,128)(2,1)} %bitcast.8, bf16[64,1792]{1,0:T(8,128)(2,1)} %bitcast.9, bf16[64,512]{1,0:T(8,128)(2,1)} %bitcast.10, bf16[640,4096]{1,0:T(8,128)(2,1)} %bitcast.7, s32[4,64]{1,0:T(4,128)} %bitcast.11), custom_call_target="tpu_custom_call" | custom-call | tf_op jit(solution)/shard_map/attribution/pallas_call | solution.py:461
  66.6 3.1 %pick.1 = f32[64,4,640]{2,1,0:T(4,128)} custom-call(s32[4,64]{1,0:T(4,128)} %bitcast.12, bf16[8,4,104,128]{3,2,1,0:T(8,128)(2,1)} %attribution.1.ret), custom_call_target="tpu_custom_call" | custom-call | tf_op jit(solution)/shard_map/pick/pallas_call | solution.py:504
